TPU v7x, 32 devices: a whole 2x2x4 slice. The times are simulated.
32 devices in a mesh: groups: 2 (over x), fibre: 16 (over z, y, core).
Axes of the slice: x: 2, y: 2, z: 4, core: 2. Of those that a mesh axis runs over, the one named last changes fastest.
Arguments:
- traces: bfloat16 [2048, 4096], P(('groups', 'fibre')), parts along dimension 0, may hold values from -6 to 6
- alive: int32 [2048], P(('groups', 'fibre')), parts along dimension 0, may hold values 0 or 1
- offsets: int32 [3], replicated, may hold values from 1 to 256, as said below
- probe: bfloat16 [4096, 64], replicated, may hold values from -0.09375 to 0.09375
Outputs:
- correlations: bfloat16 [3, 2048, 4096], P(None, ('groups', 'fibre')), parts along dimension 1
- denoised: bfloat16 [3, 2048, 4096], P(None, ('groups', 'fibre')), parts along dimension 1
There are 2 independent parts, one for each index of `groups`. A program takes and returns all parts, laid end to end along the dimension named above; an argument that names none is the same for every part. Nothing has to cross between parts.
Inputs may be any that keep to these rules, and one draw needn't show every extreme that they name: 3 distinct offsets, one of them equal to 256.
All inputs are finite; a program needn't handle non-finite values. No bound on the sum of `alive` on one device may be relied on, other than what follows from the above.
Results may differ from a plain program's by a relative error of at most 0.028.
Values may be sent and summed in bfloat16 or wider, within the bound.
A program may use at most 64 MiB of HBM per device.

v0:
```python
import math

import jax
import jax.numpy as jnp
from jax import lax
from jax.sharding import PartitionSpec as P

ROOT = 64
RANK = 64
WINDOW = 256


TWO_PI = 2.0 * math.pi
HIGHEST_ACCURACY = lax.Precision.HIGHEST


def passed_along(value, axis, by):
    peers = lax.axis_size(axis)
    pairs = [(i, i + by) for i in range(peers) if 0 <= i + by < peers]
    return lax.ppermute(value, axis, pairs)


def dft_tables(root):
    index = jnp.arange(root, dtype=jnp.int32)
    matrix_product = index[:, None] * index[None, :]
    angle = TWO_PI * (matrix_product % root).astype(jnp.float32) / root
    twist = TWO_PI * matrix_product.astype(jnp.float32) / (root * root)
    return (jnp.cos(angle), jnp.sin(angle), jnp.cos(twist), jnp.sin(twist))


def spectra(traces, alive, tables):
    cosine, sine, twist_cos, twist_sin = tables
    count = traces.shape[0]
    signal_traces = traces.astype(jnp.float32).reshape(count, ROOT, ROOT)
    first_real = jnp.einsum("kn,cnm->ckm", cosine, signal_traces, precision=HIGHEST_ACCURACY)
    first_imag = -jnp.einsum("kn,cnm->ckm", sine, signal_traces, precision=HIGHEST_ACCURACY)
    turned_real = first_real * twist_cos + first_imag * twist_sin
    turned_imag = first_imag * twist_cos - first_real * twist_sin
    forward_transform = jnp.concatenate(
        [jnp.concatenate([cosine, -sine], 1), jnp.concatenate([sine, cosine], 1)], 0
    )
    stacked = jnp.concatenate([turned_real, turned_imag], -1)
    spectrum = jnp.einsum("ckj,jl->ckl", stacked, forward_transform, precision=HIGHEST_ACCURACY)
    power = spectrum[..., :ROOT] ** 2 + spectrum[..., ROOT:] ** 2
    level = jnp.mean(power, axis=(1, 2), keepdims=True)
    scale = alive.astype(jnp.float32)[:, None, None] / jnp.sqrt(power + 0.1 * (level + 1e-05))
    return (spectrum * jnp.concatenate([scale, scale], -1)).astype(jnp.bfloat16)


def correlate(own, other, tables):
    cosine, sine, twist_cos, twist_sin = tables
    count = own.shape[0]
    own_wide = own.astype(jnp.float32)
    other_wide = other.astype(jnp.float32)
    own_real, own_imag = (own_wide[..., :ROOT], own_wide[..., ROOT:])
    other_real, other_imag = (other_wide[..., :ROOT], other_wide[..., ROOT:])
    cross_real = own_real * other_real + own_imag * other_imag
    cross_imag = own_imag * other_real - own_real * other_imag
    backward = jnp.concatenate(
        [jnp.concatenate([cosine, sine], 1), jnp.concatenate([-sine, cosine], 1)], 0
    )
    stacked = jnp.concatenate([cross_real, cross_imag], -1)
    inner = jnp.einsum("ckj,jl->ckl", stacked, backward, precision=HIGHEST_ACCURACY)
    inner_real, inner_imag = (inner[..., :ROOT], inner[..., ROOT:])
    turned_real = inner_real * twist_cos - inner_imag * twist_sin
    turned_imag = inner_real * twist_sin + inner_imag * twist_cos
    outer = jnp.concatenate([cosine, -sine], 1)
    joined = jnp.concatenate([turned_real, turned_imag], 1)
    lagged = jnp.einsum("mk,ckn->cmn", outer, joined, precision=HIGHEST_ACCURACY)
    return lagged.reshape(count, ROOT * ROOT) * (1.0 / ROOT)


def body(traces, alive, offsets, probe):
    count, total = traces.shape
    tables = dft_tables(ROOT)
    own = spectra(traces, alive, tables)
    hops = WINDOW // count
    blocks = [own]
    for step in range(1, hops + 1):
        blocks.append(passed_along(own, "fibre", -step))
    extended = jnp.concatenate(blocks, axis=0)
    eye_rank = jnp.eye(RANK, dtype=jnp.float32)

    def panel_for(offset):
        other = lax.dynamic_slice_in_dim(extended, offset, count, 0)
        panel = correlate(own, other, tables).astype(jnp.bfloat16)
        sketch = jnp.dot(panel, probe, preferred_element_type=jnp.float32).astype(jnp.bfloat16)
        gram = jnp.dot(sketch.T, sketch, preferred_element_type=jnp.float32)
        return (panel, sketch, gram)

    def project(weight_factors, moments):
        return jnp.dot(weight_factors, moments.T, precision=HIGHEST_ACCURACY).astype(jnp.bfloat16)

    panels, random_sketches, grams = lax.map(panel_for, offsets)
    moments = jnp.einsum(
        "ocn,ocr->onr", panels, random_sketches, preferred_element_type=jnp.float32
    )
    grams, moments = (
        lax.psum(grams.astype(jnp.bfloat16), "fibre").astype(jnp.float32),
        lax.psum(moments.astype(jnp.bfloat16), "fibre").astype(jnp.float32),
    )
    factor = jnp.linalg.cholesky(grams)
    inverse_transform = jax.vmap(lambda lower: jax.scipy.linalg.cho_solve((lower, True), eye_rank))(
        factor
    )
    weight_factors = jnp.einsum(
        "nhk,nkd->nhd",
        random_sketches.astype(jnp.float32),
        inverse_transform,
        precision=HIGHEST_ACCURACY,
    )
    denoised = lax.map(lambda pair: project(pair[0], pair[1]), (weight_factors, moments))
    return (panels, denoised)


def solution(mesh):
    placed = (P(("groups", "fibre"), None), P(("groups", "fibre")), P(), P())
    return jax.shard_map(
        body,
        mesh=mesh,
        in_specs=placed,
        out_specs=(P(None, ("groups", "fibre"), None), P(None, ("groups", "fibre"), None)),
        check_vma=False,
    )
```

profile of v0, /device:TPU:0, one launch (start us, length us, event | category | flops | bytes accessed | tf_op | source)
XLA Modules:
  0.0 278.1 jit_solution(11146675847766730965)
XLA Ops:
  7.6 2.1 reshape.81
  12.5 1.9 fusion.32
  16.7 1.7 constant_dynamic-update-slice_fusion.5
  23.8 2.3 constant_dynamic-update-slice_fusion.4
  26.1 42.0 %collective-permute-done.1 = bf16[64,64,128]{2,1,0:T(8,128)(2,1)} collective-permute-done((bf16[64,64,128]{2,1,0:T(8,128)(2,1)S(1)}, bf16[64,64,128]{2,1,0:T(8,128)(2,1)}, u32[]{:S(2)}, u32[]{:S(2)}) %collective-permute-start.1) | collective-permute-done | bytes 1048608 | tf_op jit(solution)/shard_map/ppermute | solution.py:20
  68.1 2.3 constant_dynamic-update-slice_fusion.3
  71.4 32.9 %collective-permute-done.3 = bf16[64,64,128]{2,1,0:T(8,128)(2,1)S(1)} collective-permute-done((bf16[64,64,128]{2,1,0:T(8,128)(2,1)S(1)}, bf16[64,64,128]{2,1,0:T(8,128)(2,1)S(1)}, u32[]{:S(2)}, u32[]{:S(2)}) %collective-permute-start.3) | collective-permute-done | bytes 1048608 | tf_op jit(solution)/shard_map/ppermute | solution.py:20
  106.7 56.8 %while.29 = (s32[]{:T(128)}, bf16[3,64,4096]{2,1,0:T(8,128)(2,1)}, bf16[3,64,64]{2,1,0:T(8,128)(2,1)S(1)}, bf16[3,64,64]{1,2,0:T(8,128)(2,1)S(1)}, bf16[64,64,12...) while((s32[]{:T(128)}, bf16[3,64,4096]{2,1,0:T(8,128)(2,1)}, ...), condition=%wide.region_2.3_spmd.clone.clone, body=%wide.region_1.2_spmd.clone.clone.sunk | while | flops 1247821824 | bytes 31195860 | solution.py:94
  112.3 1.9 fusion.118
  115.2 6.7 %fusion.120 = bf16[64,64,64]{1,2,0:T(8,128)(2,1)S(1)} fusion(f32[64,64,64]{2,1,0:T(8,128)S(1)} %get-tuple-element.387, f32[64,64,64]{2,1,0:T(8,128)S(1)} %get-tuple-element.388, f32[64,128]{1,0:T(8,128)S(1)} %get-tuple-element.425), kind=kOutput, calls=%fused_computation.23.clone.1 | convolution fusion | flops 403701760 | bytes 2654208 | tf_op jit(solution)/shard_map/while/body/eval_jaxpr/mk,ckn->cmn/dot_general | solution.py:69
  131.2 1.9 fusion.118
  134.1 6.7 %fusion.120 = bf16[64,64,64]{1,2,0:T(8,128)(2,1)S(1)} fusion(f32[64,64,64]{2,1,0:T(8,128)S(1)} %get-tuple-element.387, f32[64,64,64]{2,1,0:T(8,128)S(1)} %get-tuple-element.388, f32[64,128]{1,0:T(8,128)S(1)} %get-tuple-element.425), kind=kOutput, calls=%fused_computation.23.clone.1 | convolution fusion | flops 403701760 | bytes 2654208 | tf_op jit(solution)/shard_map/while/body/eval_jaxpr/mk,ckn->cmn/dot_general | solution.py:69
  150.1 1.9 fusion.118
  153.0 6.7 %fusion.120 = bf16[64,64,64]{1,2,0:T(8,128)(2,1)S(1)} fusion(f32[64,64,64]{2,1,0:T(8,128)S(1)} %get-tuple-element.387, f32[64,64,64]{2,1,0:T(8,128)S(1)} %get-tuple-element.388, f32[64,128]{1,0:T(8,128)S(1)} %get-tuple-element.425), kind=kOutput, calls=%fused_computation.23.clone.1 | convolution fusion | flops 403701760 | bytes 2654208 | tf_op jit(solution)/shard_map/while/body/eval_jaxpr/mk,ckn->cmn/dot_general | solution.py:69
  163.5 3.2 %convolution_convert_fusion.2 = bf16[3,4096,64]{1,2,0:T(8,128)(2,1)} fusion(bf16[3,64,4096]{2,1,0:T(8,128)(2,1)} %get-tuple-element.173, bf16[3,64,64]{2,1,0:T(8,128)(2,1)S(1)} %get-tuple-element.176), kind=kOutput, calls=%fused_computation.37 | convolution fusion | flops 101449728 | bytes 3170304 | tf_op jit(solution)/shard_map/ocn,ocr->onr/dot_general | solution.py:95
  166.7 58.3 %psum.14 = bf16[3,64,64]{1,2,0:T(8,128)(2,1)S(1)} all-reduce(bf16[3,64,64]{1,2,0:T(8,128)(2,1)S(1)} %get-tuple-element.177), channel_id=1, replica_groups=mesh['groups'=2,'fibre'=16] {'fibre'}, use_global_device_ids=true, to_apply=%region_3.4 | all-reduce | flops 12288 | bytes 49152 | tf_op jit(solution)/shard_map/psum | solution.py:99
  225.1 17.6 %custom-call.11 = f32[3,64,64]{2,1,0:T(8,128)S(1)} custom-call(f32[3,64,64]{2,1,0:T(8,128)S(1)} %fusion.42), custom_call_target="Cholesky" | custom-call | tf_op jit(solution)/shard_map/jit(cholesky)/cholesky | solution.py:102
  243.0 14.7 %custom-call.12 = f32[3,1,64,64]{2,3,1,0:T(8,128)S(1)} custom-call(f32[3,1,64,64]{3,2,1,0:T(8,128)S(1)} %select_bitcast_fusion), custom_call_target="InvertDiagBlocksLowerTriangular" | custom-call | tf_op jit(solution)/shard_map/vmap(jit(_cho_solve))/triangular_solve | solution.py:103
  258.5 4.3 %all-reduce.2.cloned.1.call-done = bf16[3,4096,64]{1,2,0:T(8,128)(2,1)} async-done(((bf16[3,4096,64]{1,2,0:T(8,128)(2,1)}), bf16[3,4096,64]{1,2,0:T(8,128)(2,1)}) %all-reduce.2.cloned.1.call-update) | async-done | bytes 1572880 | tf_op jit(solution)/shard_map/psum | solution.py:100
  262.8 1.7 convert_element_type.118
  265.8 5.4 %while.28 = (s32[]{:T(128)}, bf16[3,64,4096]{2,1,0:T(8,128)(2,1)}, f32[3,64,64]{2,1,0:T(8,128)S(1)}, f32[3,4096,64]{1,2,0:T(8,128)S(1)}, s32[]{:T(128)}) while((s32[]{:T(128)}, bf16[3,64,4096]{2,1,0:T(8,128)(2,1)}, f32[3,64,64]{2,1,0:T(8,128)S(1)}, f32[3,4096,64]{1,2,0:T(8,128)S(1)}, s32[]{:T(128)}) %tuple.70), condition=%wide.region_8.9_spmd, body=%wide.region_7.8_spmd.sunk | while | flops 201588736 | bytes 1607229 | solution.py:112
  265.8 1.8 fusion.109
  267.7 1.8 fusion.109
  269.5 1.8 fusion.109
  (82 shorter events, 42.0 us)
Async XLA Ops:
  7.2 255.6 %all-reduce.2.cloned.1.call-start = ((), (), s32[]{:S(2)}) async-start(), calls=%async_computation | async-start | bytes 3145728 | tf_op jit(solution)/shard_map/psum | solution.py:100
  14.4 1.5 copy-start.1
  18.4 5.4 %collective-permute-start = (bf16[64,64,128]{2,1,0:T(8,128)(2,1)S(1)}, bf16[64,64,128]{2,1,0:T(8,128)(2,1)}, u32[]{:S(2)}, u32[]{:S(2)}) collective-permute-start(bf16[64,64,128]{2,1,0:T(8,128)(2,1)S(1)} %get-tuple-element.395), channel_id=1, source_target_pairs={{1,0},{2,1},{3,2},{4,3},{5,4},{6,5},{7,6},{8,7},{9,8},{10,9},{11,1... | collective-permute-start | bytes 3145736 | tf_op jit(solution)/shard_map/ppermute | solution.py:20
  19.7 48.4 %collective-permute-start.1 = (bf16[64,64,128]{2,1,0:T(8,128)(2,1)S(1)}, bf16[64,64,128]{2,1,0:T(8,128)(2,1)}, u32[]{:S(2)}, u32[]{:S(2)}) collective-permute-start(bf16[64,64,128]{2,1,0:T(8,128)(2,1)S(1)} %get-tuple-element.395), channel_id=1, source_target_pairs={{2,0},{3,1},{4,2},{5,3},{6,4},{7,5},{8,6},{9,7},{10,8},{11,9},{12,... | collective-permute-start | bytes 3145736 | tf_op jit(solution)/shard_map/ppermute | solution.py:20
  21.0 49.4 %collective-permute-start.2 = (bf16[64,64,128]{2,1,0:T(8,128)(2,1)S(1)}, bf16[64,64,128]{2,1,0:T(8,128)(2,1)S(1)}, u32[]{:S(2)}, u32[]{:S(2)}) collective-permute-start(bf16[64,64,128]{2,1,0:T(8,128)(2,1)S(1)} %get-tuple-element.395), channel_id=1, source_target_pairs={{3,0},{4,1},{5,2},{6,3},{7,4},{8,5},{9,6},{10,7},{11,8},{12,9},{13... | collective-permute-start | bytes 3145736 | tf_op jit(solution)/shard_map/ppermute | solution.py:20
  22.3 82.1 %collective-permute-start.3 = (bf16[64,64,128]{2,1,0:T(8,128)(2,1)S(1)}, bf16[64,64,128]{2,1,0:T(8,128)(2,1)S(1)}, u32[]{:S(2)}, u32[]{:S(2)}) collective-permute-start(bf16[64,64,128]{2,1,0:T(8,128)(2,1)S(1)} %get-tuple-element.395), channel_id=1, source_target_pairs={{4,0},{5,1},{6,2},{7,3},{8,4},{9,5},{10,6},{11,7},{12,8},{13,9},{1... | collective-permute-start | bytes 3145736 | tf_op jit(solution)/shard_map/ppermute | solution.py:20
  71.4 35.3 %copy-start.2 = (s32[3]{0:T(128)S(1)}, s32[3]{0:T(128)}, u32[]{:S(2)}) copy-start(s32[3]{0:T(128)} %param.10) | copy-start | bytes 40
  122.6 2.5 copy-start
  141.4 2.5 copy-start
  160.3 2.5 copy-start
Sparse Core Ops, SparseCore 0:
  166.9 95.8 all-reduce.1
where the time goes:
time: 279 us; the launch traced here: 278 us
  waiting for transfers between devices  79.2 us (28%)
  blocking collectives  58.3 us (21%)
  other arithmetic  51.6 us (18%)
  matrix products  41.3 us (15%)
  local copies, waits for them, and re-layouts  22.6 us (8%)
  between operations  14.2 us (5%)
  loops' own time  5.67 us (2%)
  starting transfers between devices  5.19 us (2%)
    ppermute x4, waiting for transfers between devices, passed_along(): return lax.ppermute(value, axis, pairs)  74.9 us
    psum x1, blocking collectives, body(): lax.psum(grams.astype(jnp.bfloat16), 'fibre').astype(jnp.float32)  58.3 us
    dot_general x3, matrix products, correlate(): jnp.einsum('mk,ckn->cmn', outer, joined, precision=HIGHEST_ACCURACY)  20 us
    another operation x4, other arithmetic, body(): factor = jnp.linalg.cholesky(grams)  17.7 us
    another operation x3, other arithmetic, body(): jax.scipy.linalg.cho_solve((lower, True), eye_rank)  14.8 us
    convert_element_type x9, local copies, waits for them, and re-layouts, panel_for(): panel = correlate(own, other, tables).astype(jnp.bfloat16)  6.82 us
    dot_general x3, matrix products, correlate(): jnp.einsum('ckj,jl->ckl', stacked, backward, precision=HIGHEST_ACCURACY)  5.78 us
    another operation x1, loops' own time, body(): panels, random_sketches, grams = lax.map(panel_for, offsets)  5.67 us
  transfers between devices with their start and end apart: 5, of which 3 were waited for; matrix products, arithmetic and copies ran while one was open for 14% of the time, Pallas kernels for 0%

commit v1 on v0

v1 whole, which is shorter than its diff:
```python
import functools
import math

import jax
import jax.numpy as jnp
import numpy as np
from jax import lax
from jax.experimental import pallas as pl
from jax.experimental.pallas import tpu as pltpu
from jax.sharding import PartitionSpec as P

RANK = 64
WINDOW = 256
LANES = 128
ROWS = 16
F32 = jnp.float32
BF16 = jnp.bfloat16
MESH = pl.DeviceIdType.MESH


def tables(total):
    radix = total // LANES
    half = radix // 2 + 1
    n = np.arange(LANES)
    angle = 2.0 * math.pi * ((n[:, None] * n[None, :]) % LANES) / LANES
    cosine, sine = np.cos(angle), np.sin(angle)
    forward = np.block([[cosine, -sine], [sine, cosine]])
    backward = np.block([[cosine, sine], [-sine, cosine]])
    twist = 2.0 * math.pi * np.arange(half)[:, None] * n[None, :] / total
    twists = np.stack([np.cos(twist), np.sin(twist)])[:, :, None, :]
    return (
        jnp.asarray(forward, BF16),
        jnp.asarray(backward, BF16),
        jnp.asarray(twists, F32),
    )


def add(a, b):
    return b if a is None else (a if b is None else a + b)


def sub(a, b):
    if b is None:
        return a
    return -b if a is None else a - b


def turn(value, k, n, sign):
    re, im = value
    if k == 0:
        return value
    c, s = math.cos(2 * math.pi * k / n), sign * math.sin(2 * math.pi * k / n)
    if abs(c) < 1e-12:
        if s > 0:
            return (None if im is None else -im, re)
        return (im, None if re is None else -re)
    if im is None:
        return (re * c, re * s)
    if abs(abs(c) - abs(s)) < 1e-12:
        r = abs(c)
        a, b = math.copysign(1, c), math.copysign(1, s)
        x = (re if a > 0 else -re) - (im if b > 0 else -im)
        y = (re if b > 0 else -re) + (im if a > 0 else -im)
        return (x * r, y * r)
    return (re * c - im * s, re * s + im * c)


def real_forward(x):
    n = len(x)
    if n == 1:
        return [(x[0], None)]
    if n == 2:
        return [(x[0] + x[1], None), (x[0] - x[1], None)]
    even, odd = real_forward(x[0::2]), real_forward(x[1::2])
    out = [None] * (n // 2 + 1)
    for k in range(n // 4 + 1):
        e, o = even[k], turn(odd[k], k, n, -1.0)
        out[k] = (add(e[0], o[0]), add(e[1], o[1]))
        if n // 2 - k != k:
            low = (sub(e[0], o[0]), sub(e[1], o[1]))
            out[n // 2 - k] = (low[0], None if low[1] is None else -low[1])
    return out


def real_backward(v):
    n = 2 * (len(v) - 1)
    if n == 2:
        return [v[0][0] + v[1][0], v[0][0] - v[1][0]]
    even, odd = [], []
    for k in range(n // 4 + 1):
        a, b = v[k], v[n // 2 - k]
        if k == 0:
            even.append((a[0] + b[0], None))
            odd.append((a[0] - b[0], None))
        elif k == n // 4:
            even.append((a[0] + a[0], None))
            odd.append((-(a[1] + a[1]), None))
        else:
            even.append((a[0] + b[0], a[1] - b[1]))
            odd.append(turn((a[0] - b[0], a[1] + b[1]), k, n, 1.0))
    out = [None] * n
    out[0::2] = real_backward(even)
    out[1::2] = real_backward(odd)
    return out


def spectra_kernel(
    peers, chunks, x_ref, alive_ref, forward_ref, twist_ref, slots, turned, level,
    core_s, core_r, z_s, z_r, y_s, y_r, relay_s, relay_r, done_s, done_r,
):
    count, total = x_ref.shape
    radix = total // LANES
    half = radix // 2 + 1
    me = lax.axis_index("fibre")
    core = lax.rem(me, 2)
    chip = me // 2
    odd = lax.rem(chip, 2)
    pair = me + 1 - 2 * core
    across = me + 2 - 4 * odd
    upper, lower = me + 4, me - 4
    has_upper, has_lower = me < peers - 4, me >= 4
    barrier = pltpu.get_barrier_semaphore()
    for peer in (pair, across):
        pl.semaphore_signal(barrier, inc=1, device_id={"fibre": peer}, device_id_type=MESH)

    @pl.when(has_upper)
    def _():
        pl.semaphore_signal(barrier, inc=1, device_id={"fibre": upper}, device_id_type=MESH)

    @pl.when(has_lower)
    def _():
        pl.semaphore_signal(barrier, inc=1, device_id={"fibre": lower}, device_id_type=MESH)

    @pl.loop(0, count // ROWS)
    def _(step):
        rows = pl.ds(pl.multiple_of(step * ROWS, ROWS), ROWS)
        x = [x_ref[rows, a * LANES : (a + 1) * LANES].astype(F32) for a in range(radix)]
        squares = x[0] * x[0]
        for a in range(1, radix):
            squares = squares + x[a] * x[a]
        energy = jnp.sum(squares, axis=1, keepdims=True)
        level[rows, :] = jnp.broadcast_to(0.1 * (energy + 1e-05), (ROWS, LANES))
        for k, (re, im) in enumerate(real_forward(x)):
            cosine, sine = twist_ref[0, k], twist_ref[1, k]
            if im is None:
                turned[k, rows, :LANES] = (re * cosine).astype(BF16)
                turned[k, rows, LANES:] = (-(re * sine)).astype(BF16)
            else:
                turned[k, rows, :LANES] = (re * cosine + im * sine).astype(BF16)
                turned[k, rows, LANES:] = (im * cosine - re * sine).astype(BF16)

    shape = (count, count)
    eye = lax.broadcasted_iota(jnp.int32, shape, 0) == lax.broadcasted_iota(jnp.int32, shape, 1)
    alive = jnp.where(eye, jnp.broadcast_to(alive_ref[...].astype(F32), shape), 0.0)
    alive = jnp.broadcast_to(jnp.sum(alive, axis=1, keepdims=True), (count, LANES))

    met = 2 + has_upper.astype(jnp.int32) + has_lower.astype(jnp.int32)
    pl.semaphore_wait(barrier, met)

    def move(source, target, part, send, recv, index, peer):
        lo, hi = part
        return pltpu.make_async_remote_copy(
            src_ref=slots.at[source, pl.ds(lo, hi - lo)],
            dst_ref=slots.at[target, pl.ds(lo, hi - lo)],
            send_sem=send.at[index],
            recv_sem=recv.at[index],
            device_id={"fibre": peer},
            device_id_type=MESH,
        )

    own, nearer, farther = core, 2 + core, 4 + core
    for index, part in enumerate(chunks):
        for k in range(*part):
            spectrum = jnp.dot(turned[k], forward_ref[...], preferred_element_type=F32)
            re, im = spectrum[:, :LANES], spectrum[:, LANES:]
            scale = alive * lax.rsqrt(re * re + im * im + level[...])
            slots[own, k, :, :LANES] = (re * scale).astype(BF16)
            slots[own, k, :, LANES:] = (im * scale).astype(BF16)

        @pl.when(has_lower)
        def _():
            move(own, farther, part, z_s, z_r, index, lower).start()

        @pl.when(odd == 1)
        def _():
            move(own, nearer, part, y_s, y_r, index, across).start()

        move(own, own, part, core_s, core_r, index, pair).start()

    @pl.when(jnp.logical_not(has_upper))
    def _():
        for k in range(half):
            slots[farther, k] = jnp.zeros((count, 2 * LANES), BF16)

    for index, part in enumerate(chunks):
        @pl.when(has_upper)
        def _():
            move(own, farther, part, z_s, z_r, index, lower).wait_recv()

        @pl.when(odd == 0)
        def _():
            move(farther, nearer, part, y_s, y_r, index, across).start()

        move(farther, farther, part, done_s, done_r, index, pair).start()
        move(own, nearer, part, y_s, y_r, index, across).wait_recv()
        move(nearer, nearer, part, relay_s, relay_r, index, pair).start()
    for index, part in enumerate(chunks):
        move(own, own, part, core_s, core_r, index, pair).wait()
        move(farther, farther, part, done_s, done_r, index, pair).wait()
        move(nearer, nearer, part, relay_s, relay_r, index, pair).wait()
        move(own, nearer, part, y_s, y_r, index, across).wait_send()

        @pl.when(has_lower)
        def _():
            move(own, farther, part, z_s, z_r, index, lower).wait_send()


def spectra(traces, alive, forward, twists, peers):
    count, total = traces.shape
    half = total // LANES // 2 + 1
    pieces = 4
    cuts = [half * i // pieces for i in range(pieces + 1)]
    chunks = tuple(zip(cuts[:-1], cuts[1:]))
    vmem = pl.BlockSpec(memory_space=pltpu.VMEM)
    return pl.pallas_call(
        functools.partial(spectra_kernel, peers, chunks),
        name="spectra",
        out_shape=jax.ShapeDtypeStruct((6, half, count, 2 * LANES), BF16),
        in_specs=[vmem] * 4,
        out_specs=vmem,
        scratch_shapes=[
            pltpu.VMEM((half, count, 2 * LANES), BF16),
            pltpu.VMEM((count, LANES), F32),
        ]
        + [pltpu.SemaphoreType.DMA((pieces,))] * 10,
        compiler_params=pltpu.CompilerParams(collective_id=0, has_side_effects=True),
    )(traces, alive.reshape(1, count), forward, twists)


def panel_kernel(
    offsets_ref, slots, backward_ref, twist_ref, probe_ref, panel_ref, sketch_ref, gram_ref,
    moment_ref, cross, wide,
):
    half, count = slots.shape[1], slots.shape[2]
    radix = 2 * (half - 1)
    total = radix * LANES
    core = lax.rem(lax.axis_index("fibre"), 2)
    start = core * count + offsets_ref[pl.program_id(0)]
    block = start // count
    shift = start - block * count
    after = jnp.minimum(block + 1, 5)
    shape = (count, count)
    gap = lax.broadcasted_iota(jnp.int32, shape, 1) - lax.broadcasted_iota(jnp.int32, shape, 0)
    first = jnp.where(gap == shift, 1.0, 0.0).astype(BF16)
    second = jnp.where(gap == shift - count, 1.0, 0.0).astype(BF16)
    pick = jnp.concatenate([first, second], axis=1)
    for k in range(half):
        both = jnp.concatenate([slots[block, k], slots[after, k]], axis=0)
        other = jnp.dot(pick, both, preferred_element_type=F32)
        own = slots[core, k].astype(F32)
        a, b = own[:, :LANES], own[:, LANES:]
        c, d = other[:, :LANES], other[:, LANES:]
        cross[k, :, :LANES] = (a * c + b * d).astype(BF16)
        cross[k, :, LANES:] = (b * c - a * d).astype(BF16)
    for k in range(half):
        inner = jnp.dot(cross[k], backward_ref[...], preferred_element_type=F32)
        re, im = inner[:, :LANES], inner[:, LANES:]
        cosine, sine = twist_ref[0, k], twist_ref[1, k]
        wide[k, :, :LANES] = re * cosine - im * sine
        if 0 < k < half - 1:
            wide[k, :, LANES:] = re * sine + im * cosine

    @pl.loop(0, count // ROWS)
    def _(step):
        rows = pl.ds(pl.multiple_of(step * ROWS, ROWS), ROWS)
        values = []
        for k in range(half):
            inside = 0 < k < half - 1
            values.append((wide[k, rows, :LANES], wide[k, rows, LANES:] if inside else None))
        for a, out in enumerate(real_backward(values)):
            panel_ref[0, rows, a * LANES : (a + 1) * LANES] = (out * total**-0.5).astype(BF16)

    sketch = jnp.dot(panel_ref[0], probe_ref[...], preferred_element_type=F32)
    flipped = sketch.T.astype(BF16)
    sketch = sketch.astype(BF16)
    sketch_ref[0] = sketch
    gram_ref[0] = jnp.dot(flipped, sketch, preferred_element_type=F32)
    parts, width = moment_ref.shape[1], moment_ref.shape[3]
    for p in range(parts):
        columns = panel_ref[0, :, p * width : (p + 1) * width]
        moment_ref[0, p] = jnp.dot(flipped, columns, preferred_element_type=F32).astype(BF16)


def panels(offsets, slots, backward, twists, probe, peers):
    _, half, count, _ = slots.shape
    total = probe.shape[0]
    many = offsets.shape[0]
    vmem = pl.BlockSpec(memory_space=pltpu.VMEM)
    width = total // peers

    def per(*shape):
        return pl.BlockSpec((1,) + shape, lambda o: (o,) + (0,) * len(shape))

    return pl.pallas_call(
        panel_kernel,
        name="panels",
        grid=(many,),
        out_shape=(
            jax.ShapeDtypeStruct((many, count, total), BF16),
            jax.ShapeDtypeStruct((many, count, RANK), BF16),
            jax.ShapeDtypeStruct((many, RANK, RANK), F32),
            jax.ShapeDtypeStruct((many, peers, RANK, width), BF16),
        ),
        in_specs=[pl.BlockSpec(memory_space=pltpu.SMEM)] + [vmem] * 4,
        out_specs=(per(count, total), per(count, RANK), per(RANK, RANK), per(peers, RANK, width)),
        scratch_shapes=[
            pltpu.VMEM((half, count, 2 * LANES), BF16),
            pltpu.VMEM((half, count, 2 * LANES), F32),
        ],
    )(offsets, slots, backward, twists, probe)


def eliminate(matrix, pivots):
    shape = matrix.shape
    row_at = lax.broadcasted_iota(jnp.int32, shape, 1)
    column_at = lax.broadcasted_iota(jnp.int32, shape, 2)
    for k in pivots:
        row = matrix[:, k : k + 1, :]
        on_column = column_at == k
        column = jnp.sum(jnp.where(on_column, matrix, 0.0), axis=2, keepdims=True)
        pivot = 1.0 / column[:, k : k + 1, :]
        scaled = jnp.where(on_column[:, :1, :], pivot, row * pivot)
        matrix = jnp.where(
            row_at == k, scaled, jnp.where(on_column, 0.0, matrix) - column * scaled
        )
    return matrix


def orders(peers, many):
    bits = [1 << i for i in range(peers.bit_length() - 1)]
    return [bits for _ in range(many)]


def reduce_kernel(
    peers, moment_ref, gram_ref, full, inverse_ref, sums, landed, grams, gram_in,
    rs_s, rs_r, ag_s, ag_r, g_s, g_r,
):
    many = moment_ref.shape[0]
    plan = orders(peers, many)
    steps = len(plan[0])
    me = lax.axis_index("fibre")

    def bit_of(bit):
        return lax.rem(me // bit, 2)

    def partner(bit):
        return me + bit - 2 * bit * bit_of(bit)

    barrier = pltpu.get_barrier_semaphore()
    for bit in plan[0]:
        pl.semaphore_signal(barrier, inc=1, device_id={"fibre": partner(bit)}, device_id_type=MESH)
    pl.semaphore_wait(barrier, steps)

    def remote(src, dst, send, recv, peer):
        return pltpu.make_async_remote_copy(
            src_ref=src, dst_ref=dst, send_sem=send, recv_sem=recv,
            device_id={"fibre": peer}, device_id_type=MESH,
        )

    low = [[0] for _ in range(many)]
    for o in range(many):
        for s in range(steps):
            low[o].append(low[o][s] + bit_of(plan[o][s]) * (peers >> (s + 1)))
    base = [peers - (peers >> s) for s in range(steps)]

    def halve(o, s):
        size = peers >> (s + 1)
        bit = plan[o][s]
        theirs = low[o][s] + (1 - bit_of(bit)) * size
        source = moment_ref if s == 0 else sums
        return remote(
            source.at[o, pl.ds(theirs, size)], landed.at[o, pl.ds(base[s], size)],
            rs_s.at[o, s], rs_r.at[o, s], partner(bit),
        )

    def double(s):
        source = gram_ref if s == 0 else grams.at[s]
        return remote(source, gram_in.at[s], g_s.at[s], g_r.at[s], partner(plan[0][s]))

    def gather(o, s):
        size = peers >> (s + 1)
        here = full.at[o, pl.ds(low[o][s + 1], size)]
        return remote(here, here, ag_s.at[o, s], ag_r.at[o, s], partner(plan[o][s]))

    double(0).start()
    for o in range(many):
        halve(o, 0).start()
    for s in range(steps):
        size = peers >> (s + 1)
        last = s == steps - 1
        double(s).wait_recv()
        before = gram_ref[...] if s == 0 else grams[s]
        total = before + gram_in[s]
        if last:
            matrix = total
        else:
            grams[s + 1] = total
            double(s + 1).start()
        for o in range(many):
            halve(o, s).wait_recv()
            source = moment_ref if s == 0 else sums
            target = full if last else sums
            for p in range(size):
                at = low[o][s + 1] + p
                value = source[o, at].astype(F32) + landed[o, base[s] + p].astype(F32)
                target[o, at] = value.astype(BF16)
            if last:
                gather(o, s).start()
            else:
                halve(o, s + 1).start()
    share = -(-RANK // steps)
    for s in reversed(range(steps)):
        at = (steps - 1 - s) * share
        matrix = eliminate(matrix, range(at, min(at + share, RANK)))
        for o in range(many):
            gather(o, s).wait_recv()
            if s > 0:
                gather(o, s - 1).start()
    inverse_ref[...] = matrix
    for s in range(steps):
        double(s).wait_send()
        for o in range(many):
            halve(o, s).wait_send()
            gather(o, s).wait_send()


def reduced(moments, grams, peers):
    many = moments.shape[0]
    steps = peers.bit_length() - 1
    vmem = pl.BlockSpec(memory_space=pltpu.VMEM)
    dma = pltpu.SemaphoreType.DMA
    return pl.pallas_call(
        functools.partial(reduce_kernel, peers),
        name="reduced",
        out_shape=(
            jax.ShapeDtypeStruct(moments.shape, BF16),
            jax.ShapeDtypeStruct(grams.shape, F32),
        ),
        in_specs=[vmem] * 2,
        out_specs=(vmem, vmem),
        scratch_shapes=[
            pltpu.VMEM(moments.shape, BF16),
            pltpu.VMEM(moments.shape, BF16),
            pltpu.VMEM((steps,) + grams.shape, F32),
            pltpu.VMEM((steps,) + grams.shape, F32),
        ]
        + [dma((many, steps))] * 4
        + [dma((steps,))] * 2,
        compiler_params=pltpu.CompilerParams(collective_id=1, has_side_effects=True),
    )(moments, grams)


def project_kernel(sketch_ref, inverse_ref, moment_ref, out_ref):
    factors = jnp.dot(
        sketch_ref[0].astype(F32), inverse_ref[0],
        precision=lax.Precision.HIGHEST, preferred_element_type=F32,
    ).astype(BF16)
    parts, width = moment_ref.shape[1], moment_ref.shape[3]
    for p in range(parts):
        out_ref[0, :, p * width : (p + 1) * width] = jnp.dot(
            factors, moment_ref[0, p], preferred_element_type=F32
        ).astype(BF16)


def projected(sketches, inverses, moments):
    many, count, _ = sketches.shape
    parts, width = moments.shape[1], moments.shape[3]

    def per(*shape):
        return pl.BlockSpec((1,) + shape, lambda o: (o,) + (0,) * len(shape))

    return pl.pallas_call(
        project_kernel,
        name="projected",
        grid=(many,),
        out_shape=jax.ShapeDtypeStruct((many, count, parts * width), BF16),
        in_specs=[per(count, RANK), per(RANK, RANK), per(parts, RANK, width)],
        out_specs=per(count, parts * width),
    )(sketches, inverses, moments)


def body(traces, alive, offsets, probe):
    peers = lax.axis_size("fibre")
    count, total = traces.shape
    assert WINDOW == 4 * count and peers % 4 == 0
    forward, backward, twists = tables(total)
    slots = spectra(traces, alive, forward, twists, peers)
    correlations, sketches, grams, moments = panels(
        offsets, slots, backward, twists, probe, peers
    )
    moments, inverses = reduced(moments, grams, peers)
    return (correlations, projected(sketches, inverses, moments))


def solution(mesh):
    placed = (P(("groups", "fibre"), None), P(("groups", "fibre")), P(), P())
    return jax.shard_map(
        body,
        mesh=mesh,
        in_specs=placed,
        out_specs=(P(None, ("groups", "fibre"), None), P(None, ("groups", "fibre"), None)),
        check_vma=False,
    )
```

time: 279 us -> 87.4 us (0.31)
  Pallas kernels: 0 us -> 84.1 us
  waiting for transfers between devices: 79.2 us -> 0 us
  blocking collectives: 58.3 us -> 0 us
  other arithmetic: 51.6 us -> 0 us
  matrix products: 41.3 us -> 0 us
  local copies, waits for them, and re-layouts: 22.6 us -> 2.38 us
  between operations: 14.2 us -> 0.65 us
  loops' own time: 5.67 us -> 0 us
  starting transfers between devices: 5.19 us -> 0 us
    pallas_call x0 -> x4, Pallas kernels: none -> 84.1 us  [the longest x1 47.4 us: reduced(): pl.pallas_call(functools.partial(reduce_kernel, peers), name='reduced', o...]
    ppermute x4 -> x0, waiting for transfers between devices: 74.9 us -> none  [passed_along(): return lax.ppermute(value, axis, pairs)]
    psum x1 -> x0, blocking collectives: 58.3 us -> none  [body(): lax.psum(grams.astype(jnp.bfloat16), 'fibre').astype(jnp.float32)]
    dot_general x20 -> x0, matrix products: 40.8 us -> none  [the longest x3 20 us: correlate(): jnp.einsum('mk,ckn->cmn', outer, joined, precision=HIGHEST_ACCURACY)]
    another operation x7 -> x0, other arithmetic: 32.6 us -> none  [the longest x4 17.7 us: body(): factor = jnp.linalg.cholesky(grams)]
    convert_element_type x10 -> x0, local copies, waits for them, and re-layouts: 6.91 us -> none  [the longest x9 6.82 us: panel_for(): panel = correlate(own, other, tables).astype(jnp.bfloat16)]
    convert_element_type x9 -> x0, other arithmetic: 6.86 us -> none  [the longest x3 4.38 us: correlate(): other_wide = other.astype(jnp.float32)]
    another operation x2 -> x0, loops' own time: 5.67 us -> none  [the longest x1 5.67 us: body(): panels, random_sketches, grams = lax.map(panel_for, offsets)]
  transfers between devices with their start and end apart: 5 -> 0, of which waited for: 3 -> 0; matrix products, arithmetic and copies ran while one was open for 14% -> 0% of each run, Pallas kernels for 0% -> 0%
where the time goes in v1:
time: 87.4 us; the launch traced here: 87.1 us
  Pallas kernels  84.1 us (96%)
  local copies, waits for them, and re-layouts  2.38 us (3%)
    pallas_call x1, Pallas kernels, reduced(): pl.pallas_call(functools.partial(reduce_kernel, peers), name='reduced', o...  47.4 us
    pallas_call x1, Pallas kernels, spectra(): pl.pallas_call(functools.partial(spectra_kernel, peers, chunks), name='sp...  23.9 us
    pallas_call x1, Pallas kernels, panels(): pl.pallas_call(panel_kernel, name='panels', grid=(many,), out_shape=(jax....  8.63 us
    pallas_call x1, Pallas kernels, projected(): pl.pallas_call(project_kernel, name='projected', grid=(many,), out_shape=...  4.1 us
    unnamed x1, local copies, waits for them, and re-layouts  2.38 us

profile of v1, /device:TPU:0, one launch (start us, length us, event | category | flops | bytes accessed | tf_op | source)
XLA Modules:
  0.0 87.1 jit_solution(904823974327108756)
XLA Ops:
  0.6 2.4 %copy.9.probe_ref = bf16[4096,64]{1,0:T(8,128)(2,1)} copy(bf16[4096,64]{0,1:T(8,128)(2,1)} %param.10) | data formatting | bytes 1048576 | tf_op args[3]
  3.0 23.9 %spectra.1.slots = bf16[6,17,64,256]{3,2,1,0:T(8,128)(2,1)} custom-call(bf16[64,4096]{1,0:T(8,128)(2,1)} %x_ref.1, s32[1,64]{1,0:T(1,128)} %bitcast.1, bf16[256,256]{1,0:T(8,128)(2,1)} %constant.6.clone.forward_ref, f32[2,17,1,128]{3,2,1,0:T(1,128)} %constant.8.clone.twist_ref), custom_call_target="tpu_custom_call" | custom-call | tf_op jit(solution)/shard_map/spectra/pallas_call | solution.py:225
  27.0 8.6 %panels.1 = (bf16[3,64,4096]{2,1,0:T(8,128)(2,1)}, bf16[3,64,64]{2,1,0:T(8,128)(2,1)}, f32[3,64,64]{2,1,0:T(8,128)}, bf16[3,16,64,256]{3,2,1,0:T(8,128)(2,1)}) custom-call(s32[3]{0:T(128)} %offsets_ref.1, bf16[6,17,64,256]{3,2,1,0:T(8,128)(2,1)} %spectra.1.slots, bf16[256,256]{1,0:T(8,128)(2,1)} %constant.7.clone.backward_ref, ...), custom_call_target="tpu_custom_call" | custom-call | tf_op jit(solution)/shard_map/panels/pallas_call | solution.py:304
  35.6 47.4 %reduced.1 = (bf16[3,16,64,256]{3,2,1,0:T(8,128)(2,1)}, f32[3,64,64]{2,1,0:T(8,128)}) custom-call(bf16[3,16,64,256]{3,2,1,0:T(8,128)(2,1)} %get-tuple-element.10.moment_ref, f32[3,64,64]{2,1,0:T(8,128)} %get-tuple-element.11.gram_ref), custom_call_target="tpu_custom_call" | custom-call | tf_op jit(solution)/shard_map/reduced/pallas_call | solution.py:442
  83.0 4.1 %projected.1 = bf16[3,64,4096]{2,1,0:T(8,128)(2,1)} custom-call(bf16[3,64,64]{2,1,0:T(8,128)(2,1)} %get-tuple-element.9.sketch_ref, f32[3,64,64]{2,1,0:T(8,128)} %get-tuple-element.12.inverse_ref, bf16[3,16,64,256]{3,2,1,0:T(8,128)(2,1)} %get-tuple-element.13.moment_ref), custom_call_target="tpu_custom_call" | custom-call | tf_op jit(solution)/shard_map/projected/pallas_call | solution.py:482

commit v2 on v1

--- a/solution.py
+++ b/solution.py
@@ -13,6 +13,8 @@
 WINDOW = 256
 LANES = 128
 ROWS = 16
+SPLIT = 2
+OTHERS = (0, 3)
 F32 = jnp.float32
 BF16 = jnp.bfloat16
 MESH = pl.DeviceIdType.MESH
@@ -105,12 +107,13 @@
 
 
 def spectra_kernel(
-    peers, chunks, x_ref, alive_ref, forward_ref, twist_ref, slots, turned, level,
+    peers, x_ref, alive_ref, forward_ref, twist_ref, slots, turned, wide,
     core_s, core_r, z_s, z_r, y_s, y_r, relay_s, relay_r, done_s, done_r,
 ):
     count, total = x_ref.shape
     radix = total // LANES
     half = radix // 2 + 1
+    groups = count // ROWS
     me = lax.axis_index("fibre")
     core = lax.rem(me, 2)
     chip = me // 2
@@ -131,117 +134,114 @@
     def _():
         pl.semaphore_signal(barrier, inc=1, device_id={"fibre": lower}, device_id_type=MESH)
 
-    @pl.loop(0, count // ROWS)
-    def _(step):
-        rows = pl.ds(pl.multiple_of(step * ROWS, ROWS), ROWS)
+    shape = (count, count)
+    eye = lax.broadcasted_iota(jnp.int32, shape, 0) == lax.broadcasted_iota(jnp.int32, shape, 1)
+    alive = jnp.where(eye, jnp.broadcast_to(alive_ref[...].astype(F32), shape), 0.0)
+    alive = jnp.broadcast_to(jnp.sum(alive, axis=1, keepdims=True), (count, LANES))
+
+    def move(source, target, send, recv, index, peer):
+        return pltpu.make_async_remote_copy(
+            src_ref=slots.at[source, index],
+            dst_ref=slots.at[target, index],
+            send_sem=send.at[index],
+            recv_sem=recv.at[index],
+            device_id={"fibre": peer},
+            device_id_type=MESH,
+        )
+
+    own, nearer, farther = core, 2 + core, 4 + core
+    for index in range(groups):
+        rows = slice(index * ROWS, (index + 1) * ROWS)
         x = [x_ref[rows, a * LANES : (a + 1) * LANES].astype(F32) for a in range(radix)]
         squares = x[0] * x[0]
         for a in range(1, radix):
             squares = squares + x[a] * x[a]
         energy = jnp.sum(squares, axis=1, keepdims=True)
-        level[rows, :] = jnp.broadcast_to(0.1 * (energy + 1e-05), (ROWS, LANES))
+        level = jnp.broadcast_to(0.1 * (energy + 1e-05), (ROWS, LANES))
         for k, (re, im) in enumerate(real_forward(x)):
             cosine, sine = twist_ref[0, k], twist_ref[1, k]
             if im is None:
-                turned[k, rows, :LANES] = (re * cosine).astype(BF16)
-                turned[k, rows, LANES:] = (-(re * sine)).astype(BF16)
+                turned[k, :, :LANES] = (re * cosine).astype(BF16)
+                turned[k, :, LANES:] = (-(re * sine)).astype(BF16)
             else:
-                turned[k, rows, :LANES] = (re * cosine + im * sine).astype(BF16)
-                turned[k, rows, LANES:] = (im * cosine - re * sine).astype(BF16)
-
-    shape = (count, count)
-    eye = lax.broadcasted_iota(jnp.int32, shape, 0) == lax.broadcasted_iota(jnp.int32, shape, 1)
-    alive = jnp.where(eye, jnp.broadcast_to(alive_ref[...].astype(F32), shape), 0.0)
-    alive = jnp.broadcast_to(jnp.sum(alive, axis=1, keepdims=True), (count, LANES))
-
-    met = 2 + has_upper.astype(jnp.int32) + has_lower.astype(jnp.int32)
-    pl.semaphore_wait(barrier, met)
-
-    def move(source, target, part, send, recv, index, peer):
-        lo, hi = part
-        return pltpu.make_async_remote_copy(
-            src_ref=slots.at[source, pl.ds(lo, hi - lo)],
-            dst_ref=slots.at[target, pl.ds(lo, hi - lo)],
-            send_sem=send.at[index],
-            recv_sem=recv.at[index],
-            device_id={"fibre": peer},
-            device_id_type=MESH,
-        )
-
-    own, nearer, farther = core, 2 + core, 4 + core
-    for index, part in enumerate(chunks):
-        for k in range(*part):
-            spectrum = jnp.dot(turned[k], forward_ref[...], preferred_element_type=F32)
-            re, im = spectrum[:, :LANES], spectrum[:, LANES:]
-            scale = alive * lax.rsqrt(re * re + im * im + level[...])
-            slots[own, k, :, :LANES] = (re * scale).astype(BF16)
-            slots[own, k, :, LANES:] = (im * scale).astype(BF16)
+                turned[k, :, :LANES] = (re * cosine + im * sine).astype(BF16)
+                turned[k, :, LANES:] = (im * cosine - re * sine).astype(BF16)
+        stacked = turned[...].reshape(half * ROWS, 2 * LANES)
+        wide[...] = jnp.dot(stacked, forward_ref[...], preferred_element_type=F32)
+        for k in range(half):
+            at = slice(k * ROWS, (k + 1) * ROWS)
+            re, im = wide[at, :LANES], wide[at, LANES:]
+            scale = alive[rows] * lax.rsqrt(re * re + im * im + level)
+            slots[own, index, k, :, :LANES] = (re * scale).astype(BF16)
+            slots[own, index, k, :, LANES:] = (im * scale).astype(BF16)
+        if index == 0:
+            met = 2 + has_upper.astype(jnp.int32) + has_lower.astype(jnp.int32)
+            pl.semaphore_wait(barrier, met)
 
         @pl.when(has_lower)
         def _():
-            move(own, farther, part, z_s, z_r, index, lower).start()
+            move(own, farther, z_s, z_r, index, lower).start()
 
         @pl.when(odd == 1)
         def _():
-            move(own, nearer, part, y_s, y_r, index, across).start()
-
-        move(own, own, part, core_s, core_r, index, pair).start()
+            move(own, nearer, y_s, y_r, index, across).start()
+
+        move(own, own, core_s, core_r, index, pair).start()
 
     @pl.when(jnp.logical_not(has_upper))
     def _():
-        for k in range(half):
-            slots[farther, k] = jnp.zeros((count, 2 * LANES), BF16)
-
-    for index, part in enumerate(chunks):
+        for index in range(groups):
+            for k in range(half):
+                slots[farther, index, k] = jnp.zeros((ROWS, 2 * LANES), BF16)
+
+    for index in range(groups):
         @pl.when(has_upper)
         def _():
-            move(own, farther, part, z_s, z_r, index, lower).wait_recv()
+            move(own, farther, z_s, z_r, index, lower).wait_recv()
 
         @pl.when(odd == 0)
         def _():
-            move(farther, nearer, part, y_s, y_r, index, across).start()
-
-        move(farther, farther, part, done_s, done_r, index, pair).start()
-        move(own, nearer, part, y_s, y_r, index, across).wait_recv()
-        move(nearer, nearer, part, relay_s, relay_r, index, pair).start()
-    for index, part in enumerate(chunks):
-        move(own, own, part, core_s, core_r, index, pair).wait()
-        move(farther, farther, part, done_s, done_r, index, pair).wait()
-        move(nearer, nearer, part, relay_s, relay_r, index, pair).wait()
-        move(own, nearer, part, y_s, y_r, index, across).wait_send()
+            move(farther, nearer, y_s, y_r, index, across).start()
+
+        move(farther, farther, done_s, done_r, index, pair).start()
+        move(own, nearer, y_s, y_r, index, across).wait_recv()
+        move(nearer, nearer, relay_s, relay_r, index, pair).start()
+    for index in range(groups):
+        move(own, own, core_s, core_r, index, pair).wait()
+        move(farther, farther, done_s, done_r, index, pair).wait()
+        move(nearer, nearer, relay_s, relay_r, index, pair).wait()
+        move(own, nearer, y_s, y_r, index, across).wait_send()
 
         @pl.when(has_lower)
         def _():
-            move(own, farther, part, z_s, z_r, index, lower).wait_send()
+            move(own, farther, z_s, z_r, index, lower).wait_send()
 
 
 def spectra(traces, alive, forward, twists, peers):
     count, total = traces.shape
     half = total // LANES // 2 + 1
-    pieces = 4
-    cuts = [half * i // pieces for i in range(pieces + 1)]
-    chunks = tuple(zip(cuts[:-1], cuts[1:]))
+    groups = count // ROWS
     vmem = pl.BlockSpec(memory_space=pltpu.VMEM)
     return pl.pallas_call(
-        functools.partial(spectra_kernel, peers, chunks),
+        functools.partial(spectra_kernel, peers),
         name="spectra",
-        out_shape=jax.ShapeDtypeStruct((6, half, count, 2 * LANES), BF16),
+        out_shape=jax.ShapeDtypeStruct((6, groups, half, ROWS, 2 * LANES), BF16),
         in_specs=[vmem] * 4,
         out_specs=vmem,
         scratch_shapes=[
-            pltpu.VMEM((half, count, 2 * LANES), BF16),
-            pltpu.VMEM((count, LANES), F32),
+            pltpu.VMEM((half, ROWS, 2 * LANES), BF16),
+            pltpu.VMEM((half * ROWS, 2 * LANES), F32),
         ]
-        + [pltpu.SemaphoreType.DMA((pieces,))] * 10,
+        + [pltpu.SemaphoreType.DMA((groups,))] * 10,
         compiler_params=pltpu.CompilerParams(collective_id=0, has_side_effects=True),
     )(traces, alive.reshape(1, count), forward, twists)
 
 
 def panel_kernel(
     offsets_ref, slots, backward_ref, twist_ref, probe_ref, panel_ref, sketch_ref, gram_ref,
-    moment_ref, cross, wide,
+    moment_ref, cross, inner, wide,
 ):
-    half, count = slots.shape[1], slots.shape[2]
+    half, count = slots.shape[2], slots.shape[1] * slots.shape[3]
     radix = 2 * (half - 1)
     total = radix * LANES
     core = lax.rem(lax.axis_index("fibre"), 2)
@@ -255,16 +255,20 @@
     second = jnp.where(gap == shift - count, 1.0, 0.0).astype(BF16)
     pick = jnp.concatenate([first, second], axis=1)
     for k in range(half):
-        both = jnp.concatenate([slots[block, k], slots[after, k]], axis=0)
+        flat = (count, 2 * LANES)
+        both = [slots[block, :, k].reshape(flat), slots[after, :, k].reshape(flat)]
+        both = jnp.concatenate(both, axis=0)
         other = jnp.dot(pick, both, preferred_element_type=F32)
-        own = slots[core, k].astype(F32)
+        own = slots[core, :, k].reshape(flat).astype(F32)
         a, b = own[:, :LANES], own[:, LANES:]
         c, d = other[:, :LANES], other[:, LANES:]
         cross[k, :, :LANES] = (a * c + b * d).astype(BF16)
         cross[k, :, LANES:] = (b * c - a * d).astype(BF16)
+    stacked = cross[...].reshape(half * count, 2 * LANES)
+    inner[...] = jnp.dot(stacked, backward_ref[...], preferred_element_type=F32)
     for k in range(half):
-        inner = jnp.dot(cross[k], backward_ref[...], preferred_element_type=F32)
-        re, im = inner[:, :LANES], inner[:, LANES:]
+        at = slice(k * count, (k + 1) * count)
+        re, im = inner[at, :LANES], inner[at, LANES:]
         cosine, sine = twist_ref[0, k], twist_ref[1, k]
         wide[k, :, :LANES] = re * cosine - im * sine
         if 0 < k < half - 1:
@@ -280,20 +284,25 @@
         for a, out in enumerate(real_backward(values)):
             panel_ref[0, rows, a * LANES : (a + 1) * LANES] = (out * total**-0.5).astype(BF16)
 
-    sketch = jnp.dot(panel_ref[0], probe_ref[...], preferred_element_type=F32)
+    sketch = lax.dot_general(
+        panel_ref[0], probe_ref[...], (((1,), (1,)), ((), ())), preferred_element_type=F32
+    )
     flipped = sketch.T.astype(BF16)
     sketch = sketch.astype(BF16)
     sketch_ref[0] = sketch
     gram_ref[0] = jnp.dot(flipped, sketch, preferred_element_type=F32)
-    parts, width = moment_ref.shape[1], moment_ref.shape[3]
+    split, parts, tall, width = moment_ref.shape
     for p in range(parts):
         columns = panel_ref[0, :, p * width : (p + 1) * width]
-        moment_ref[0, p] = jnp.dot(flipped, columns, preferred_element_type=F32).astype(BF16)
+        moments = jnp.dot(flipped, columns, preferred_element_type=F32).astype(BF16)
+        for h in range(split):
+            moment_ref[h, p] = moments[h * tall : (h + 1) * tall]
 
 
 def panels(offsets, slots, backward, twists, probe, peers):
-    _, half, count, _ = slots.shape
-    total = probe.shape[0]
+    _, groups, half, rows, _ = slots.shape
+    count = groups * rows
+    total = probe.shape[1]
     many = offsets.shape[0]
     vmem = pl.BlockSpec(memory_space=pltpu.VMEM)
     width = total // peers
@@ -309,12 +318,16 @@
             jax.ShapeDtypeStruct((many, count, total), BF16),
             jax.ShapeDtypeStruct((many, count, RANK), BF16),
             jax.ShapeDtypeStruct((many, RANK, RANK), F32),
-            jax.ShapeDtypeStruct((many, peers, RANK, width), BF16),
+            jax.ShapeDtypeStruct((many * SPLIT, peers, RANK // SPLIT, width), BF16),
         ),
         in_specs=[pl.BlockSpec(memory_space=pltpu.SMEM)] + [vmem] * 4,
-        out_specs=(per(count, total), per(count, RANK), per(RANK, RANK), per(peers, RANK, width)),
+        out_specs=(
+            per(count, total), per(count, RANK), per(RANK, RANK),
+            pl.BlockSpec((SPLIT, peers, RANK // SPLIT, width), lambda o: (o, 0, 0, 0)),
+        ),
         scratch_shapes=[
             pltpu.VMEM((half, count, 2 * LANES), BF16),
+            pltpu.VMEM((half * count, 2 * LANES), F32),
             pltpu.VMEM((half, count, 2 * LANES), F32),
         ],
     )(offsets, slots, backward, twists, probe)
@@ -338,7 +351,8 @@
 
 def orders(peers, many):
     bits = [1 << i for i in range(peers.bit_length() - 1)]
-    return [bits for _ in range(many)]
+    other = bits[:1] + bits[2:] + bits[1:2]
+    return [other if o in OTHERS else bits for o in range(many)]
 
 
 def reduce_kernel(
@@ -356,6 +370,10 @@
     def partner(bit):
         return me + bit - 2 * bit * bit_of(bit)
 
+    several = gram_ref.shape[0]
+    tall = several * RANK
+    loose = gram_ref[...].reshape(tall, RANK)
+    grams[0] = jnp.concatenate([loose[: tall // 2], loose[tall // 2 :]], axis=1)
     barrier = pltpu.get_barrier_semaphore()
     for bit in plan[0]:
         pl.semaphore_signal(barrier, inc=1, device_id={"fibre": partner(bit)}, device_id_type=MESH)
@@ -384,28 +402,19 @@
         )
 
     def double(s):
-        source = gram_ref if s == 0 else grams.at[s]
-        return remote(source, gram_in.at[s], g_s.at[s], g_r.at[s], partner(plan[0][s]))
+        return remote(grams.at[s], gram_in.at[s], g_s.at[s], g_r.at[s], partner(plan[0][s]))
 
     def gather(o, s):
         size = peers >> (s + 1)
         here = full.at[o, pl.ds(low[o][s + 1], size)]
         return remote(here, here, ag_s.at[o, s], ag_r.at[o, s], partner(plan[o][s]))
 
-    double(0).start()
     for o in range(many):
         halve(o, 0).start()
+    double(0).start()
     for s in range(steps):
         size = peers >> (s + 1)
         last = s == steps - 1
-        double(s).wait_recv()
-        before = gram_ref[...] if s == 0 else grams[s]
-        total = before + gram_in[s]
-        if last:
-            matrix = total
-        else:
-            grams[s + 1] = total
-            double(s + 1).start()
         for o in range(many):
             halve(o, s).wait_recv()
             source = moment_ref if s == 0 else sums
@@ -418,6 +427,14 @@
                 gather(o, s).start()
             else:
                 halve(o, s + 1).start()
+        double(s).wait_recv()
+        total = grams[s] + gram_in[s]
+        if last:
+            loose = jnp.concatenate([total[:, :RANK], total[:, RANK:]], axis=0)
+            matrix = loose.reshape(several, RANK, RANK)
+        else:
+            grams[s + 1] = total
+            double(s + 1).start()
     share = -(-RANK // steps)
     for s in reversed(range(steps)):
         at = (steps - 1 - s) * share
@@ -451,8 +468,8 @@
         scratch_shapes=[
             pltpu.VMEM(moments.shape, BF16),
             pltpu.VMEM(moments.shape, BF16),
-            pltpu.VMEM((steps,) + grams.shape, F32),
-            pltpu.VMEM((steps,) + grams.shape, F32),
+            pltpu.VMEM((steps, grams.shape[0] * RANK // 2, 2 * RANK), F32),
+            pltpu.VMEM((steps, grams.shape[0] * RANK // 2, 2 * RANK), F32),
         ]
         + [dma((many, steps))] * 4
         + [dma((steps,))] * 2,
@@ -465,10 +482,10 @@
         sketch_ref[0].astype(F32), inverse_ref[0],
         precision=lax.Precision.HIGHEST, preferred_element_type=F32,
     ).astype(BF16)
-    parts, width = moment_ref.shape[1], moment_ref.shape[3]
+    _, parts, _, width = moment_ref.shape
     for p in range(parts):
         out_ref[0, :, p * width : (p + 1) * width] = jnp.dot(
-            factors, moment_ref[0, p], preferred_element_type=F32
+            factors, moment_ref[:, p].reshape(RANK, width), preferred_element_type=F32
         ).astype(BF16)
 
 
@@ -484,7 +501,10 @@
         name="projected",
         grid=(many,),
         out_shape=jax.ShapeDtypeStruct((many, count, parts * width), BF16),
-        in_specs=[per(count, RANK), per(RANK, RANK), per(parts, RANK, width)],
+        in_specs=[
+            per(count, RANK), per(RANK, RANK),
+            pl.BlockSpec((SPLIT, parts, RANK // SPLIT, width), lambda o: (o, 0, 0, 0)),
+        ],
         out_specs=per(count, parts * width),
     )(sketches, inverses, moments)
 
@@ -496,7 +516,7 @@
     forward, backward, twists = tables(total)
     slots = spectra(traces, alive, forward, twists, peers)
     correlations, sketches, grams, moments = panels(
-        offsets, slots, backward, twists, probe, peers
+        offsets, slots, backward, twists, probe.T, peers
     )
     moments, inverses = reduced(moments, grams, peers)
     return (correlations, projected(sketches, inverses, moments))

time: 87.4 us -> 75.9 us (0.87)
  Pallas kernels: 84.1 us -> 75 us
  local copies, waits for them, and re-layouts: 2.38 us -> 0 us
    pallas_call x1, Pallas kernels: 47.4 us -> 38.4 us  [reduced(): pl.pallas_call(functools.partial(reduce_kernel, peers), name='reduced', o...]
    unnamed x1 -> x0, local copies, waits for them, and re-layouts: 2.38 us -> none
where the time goes in v2:
time: 75.9 us; the launch traced here: 75.7 us
  Pallas kernels  75 us (99%)
    pallas_call x1, Pallas kernels, reduced(): pl.pallas_call(functools.partial(reduce_kernel, peers), name='reduced', o...  38.4 us
    pallas_call x1, Pallas kernels, spectra(): pl.pallas_call(functools.partial(spectra_kernel, peers), name='spectra',...  23.8 us
    pallas_call x1, Pallas kernels, panels(): pl.pallas_call(panel_kernel, name='panels', grid=(many,), out_shape=(jax....  8.71 us
    pallas_call x1, Pallas kernels, projected(): pl.pallas_call(project_kernel, name='projected', grid=(many,), out_shape=...  4.08 us

profile of v2, /device:TPU:0, one launch (start us, length us, event | category | flops | bytes accessed | tf_op | source)
XLA Modules:
  0.0 75.7 jit_solution(12917646996741802391)
XLA Ops:
  0.6 23.8 %spectra.1.slots = bf16[6,4,17,16,256]{4,3,2,1,0:T(8,128)(2,1)} custom-call(bf16[64,4096]{1,0:T(8,128)(2,1)} %x_ref.1, s32[1,64]{1,0:T(1,128)} %bitcast.3, bf16[256,256]{1,0:T(8,128)(2,1)} %constant.6.clone.forward_ref, f32[2,17,1,128]{3,2,1,0:T(1,128)} %constant.8.clone.twist_ref), custom_call_target="tpu_custom_call" | custom-call | tf_op jit(solution)/shard_map/spectra/pallas_call | solution.py:225
  24.5 8.7 %panels.1 = (bf16[3,64,4096]{2,1,0:T(8,128)(2,1)}, bf16[3,64,64]{2,1,0:T(8,128)(2,1)}, f32[3,64,64]{2,1,0:T(8,128)}, bf16[6,16,32,256]{3,2,1,0:T(8,128)(2,1)}) custom-call(s32[3]{0:T(128)} %offsets_ref.1, bf16[6,4,17,16,256]{4,3,2,1,0:T(8,128)(2,1)} %spectra.1.slots, bf16[256,256]{1,0:T(8,128)(2,1)} %constant.7.clone.backward_ref, ...), custom_call_target="tpu_custom_call" | custom-call | tf_op jit(solution)/shard_map/panels/pallas_call | solution.py:313
  33.2 38.4 %reduced.1 = (bf16[6,16,32,256]{3,2,1,0:T(8,128)(2,1)}, f32[3,64,64]{2,1,0:T(8,128)}) custom-call(bf16[6,16,32,256]{3,2,1,0:T(8,128)(2,1)} %get-tuple-element.10.moment_ref, f32[3,64,64]{2,1,0:T(8,128)} %get-tuple-element.11.gram_ref), custom_call_target="tpu_custom_call" | custom-call | tf_op jit(solution)/shard_map/reduced/pallas_call | solution.py:459
  71.6 4.1 %projected.1 = bf16[3,64,4096]{2,1,0:T(8,128)(2,1)} custom-call(bf16[3,64,64]{2,1,0:T(8,128)(2,1)} %get-tuple-element.9.sketch_ref, f32[3,64,64]{2,1,0:T(8,128)} %get-tuple-element.12.inverse_ref, bf16[6,16,32,256]{3,2,1,0:T(8,128)(2,1)} %get-tuple-element.13.moment_ref), custom_call_target="tpu_custom_call" | custom-call | tf_op jit(solution)/shard_map/projected/pallas_call | solution.py:499

commit v3 on v2

--- a/solution.py
+++ b/solution.py
@@ -237,15 +237,15 @@
     )(traces, alive.reshape(1, count), forward, twists)
 
 
-def panel_kernel(
-    offsets_ref, slots, backward_ref, twist_ref, probe_ref, panel_ref, sketch_ref, gram_ref,
+def make_panel(
+    o, offsets_ref, slots, backward_ref, twist_ref, probe_ref, panel_ref, sketch_ref,
     moment_ref, cross, inner, wide,
 ):
     half, count = slots.shape[2], slots.shape[1] * slots.shape[3]
     radix = 2 * (half - 1)
     total = radix * LANES
     core = lax.rem(lax.axis_index("fibre"), 2)
-    start = core * count + offsets_ref[pl.program_id(0)]
+    start = core * count + offsets_ref[o]
     block = start // count
     shift = start - block * count
     after = jnp.minimum(block + 1, 5)
@@ -282,55 +282,23 @@
             inside = 0 < k < half - 1
             values.append((wide[k, rows, :LANES], wide[k, rows, LANES:] if inside else None))
         for a, out in enumerate(real_backward(values)):
-            panel_ref[0, rows, a * LANES : (a + 1) * LANES] = (out * total**-0.5).astype(BF16)
+            panel_ref[o, rows, a * LANES : (a + 1) * LANES] = (out * total**-0.5).astype(BF16)
 
     sketch = lax.dot_general(
-        panel_ref[0], probe_ref[...], (((1,), (1,)), ((), ())), preferred_element_type=F32
+        panel_ref[o], probe_ref[...], (((1,), (1,)), ((), ())), preferred_element_type=F32
     )
     flipped = sketch.T.astype(BF16)
     sketch = sketch.astype(BF16)
-    sketch_ref[0] = sketch
-    gram_ref[0] = jnp.dot(flipped, sketch, preferred_element_type=F32)
-    split, parts, tall, width = moment_ref.shape
+    sketch_ref[o] = sketch
+    gram = jnp.dot(flipped, sketch, preferred_element_type=F32)
+    parts, tall, width = moment_ref.shape[1:]
+    split = RANK // tall
     for p in range(parts):
-        columns = panel_ref[0, :, p * width : (p + 1) * width]
+        columns = panel_ref[o, :, p * width : (p + 1) * width]
         moments = jnp.dot(flipped, columns, preferred_element_type=F32).astype(BF16)
         for h in range(split):
-            moment_ref[h, p] = moments[h * tall : (h + 1) * tall]
-
-
-def panels(offsets, slots, backward, twists, probe, peers):
-    _, groups, half, rows, _ = slots.shape
-    count = groups * rows
-    total = probe.shape[1]
-    many = offsets.shape[0]
-    vmem = pl.BlockSpec(memory_space=pltpu.VMEM)
-    width = total // peers
-
-    def per(*shape):
-        return pl.BlockSpec((1,) + shape, lambda o: (o,) + (0,) * len(shape))
-
-    return pl.pallas_call(
-        panel_kernel,
-        name="panels",
-        grid=(many,),
-        out_shape=(
-            jax.ShapeDtypeStruct((many, count, total), BF16),
-            jax.ShapeDtypeStruct((many, count, RANK), BF16),
-            jax.ShapeDtypeStruct((many, RANK, RANK), F32),
-            jax.ShapeDtypeStruct((many * SPLIT, peers, RANK // SPLIT, width), BF16),
-        ),
-        in_specs=[pl.BlockSpec(memory_space=pltpu.SMEM)] + [vmem] * 4,
-        out_specs=(
-            per(count, total), per(count, RANK), per(RANK, RANK),
-            pl.BlockSpec((SPLIT, peers, RANK // SPLIT, width), lambda o: (o, 0, 0, 0)),
-        ),
-        scratch_shapes=[
-            pltpu.VMEM((half, count, 2 * LANES), BF16),
-            pltpu.VMEM((half * count, 2 * LANES), F32),
-            pltpu.VMEM((half, count, 2 * LANES), F32),
-        ],
-    )(offsets, slots, backward, twists, probe)
+            moment_ref[o * split + h, p] = moments[h * tall : (h + 1) * tall]
+    return gram
 
 
 def eliminate(matrix, pivots):
@@ -356,7 +324,8 @@
 
 
 def reduce_kernel(
-    peers, moment_ref, gram_ref, full, inverse_ref, sums, landed, grams, gram_in,
+    peers, offsets_ref, slots, backward_ref, twist_ref, probe_ref, panel_ref, sketch_ref, full,
+    inverse_ref, cross, inner, wide, moment_ref, sums, landed, grams, gram_in,
     rs_s, rs_r, ag_s, ag_r, g_s, g_r,
 ):
     many = moment_ref.shape[0]
@@ -370,14 +339,10 @@
     def partner(bit):
         return me + bit - 2 * bit * bit_of(bit)
 
-    several = gram_ref.shape[0]
-    tall = several * RANK
-    loose = gram_ref[...].reshape(tall, RANK)
-    grams[0] = jnp.concatenate([loose[: tall // 2], loose[tall // 2 :]], axis=1)
+    several = panel_ref.shape[0]
     barrier = pltpu.get_barrier_semaphore()
     for bit in plan[0]:
         pl.semaphore_signal(barrier, inc=1, device_id={"fibre": partner(bit)}, device_id_type=MESH)
-    pl.semaphore_wait(barrier, steps)
 
     def remote(src, dst, send, recv, peer):
         return pltpu.make_async_remote_copy(
@@ -409,24 +374,50 @@
         here = full.at[o, pl.ds(low[o][s + 1], size)]
         return remote(here, here, ag_s.at[o, s], ag_r.at[o, s], partner(plan[o][s]))
 
-    for o in range(many):
-        halve(o, 0).start()
-    double(0).start()
-    for s in range(steps):
+    def advance(o, s):
         size = peers >> (s + 1)
         last = s == steps - 1
+        halve(o, s).wait_recv()
+        source = moment_ref if s == 0 else sums
+        target = full if last else sums
+        for p in range(size):
+            at = low[o][s + 1] + p
+            value = source[o, at].astype(F32) + landed[o, base[s] + p].astype(F32)
+            target[o, at] = value.astype(BF16)
+        if last:
+            gather(o, s).start()
+        else:
+            halve(o, s + 1).start()
+
+    split = many // several
+    reached = [0] * many
+    loose = []
+    for panel in range(several):
+        loose.append(
+            make_panel(
+                panel, offsets_ref, slots, backward_ref, twist_ref, probe_ref, panel_ref,
+                sketch_ref, moment_ref, cross, inner, wide,
+            )
+        )
+        if panel == 0:
+            pl.semaphore_wait(barrier, steps)
+        for o in range(panel * split, (panel + 1) * split):
+            halve(o, 0).start()
+        if panel == several - 1:
+            loose = jnp.concatenate(loose, axis=0)
+            tall = several * RANK
+            grams[0] = jnp.concatenate([loose[: tall // 2], loose[tall // 2 :]], axis=1)
+            double(0).start()
+        for o in range(panel * split):
+            if reached[o] < steps - 1:
+                advance(o, reached[o])
+                reached[o] += 1
+    for s in range(steps):
+        last = s == steps - 1
         for o in range(many):
-            halve(o, s).wait_recv()
-            source = moment_ref if s == 0 else sums
-            target = full if last else sums
-            for p in range(size):
-                at = low[o][s + 1] + p
-                value = source[o, at].astype(F32) + landed[o, base[s] + p].astype(F32)
-                target[o, at] = value.astype(BF16)
-            if last:
-                gather(o, s).start()
-            else:
-                halve(o, s + 1).start()
+            if reached[o] == s:
+                advance(o, s)
+                reached[o] += 1
         double(s).wait_recv()
         total = grams[s] + gram_in[s]
         if last:
@@ -451,30 +442,42 @@
             gather(o, s).wait_send()
 
 
-def reduced(moments, grams, peers):
-    many = moments.shape[0]
+def reduced(offsets, slots, backward, twists, probe, peers):
+    _, groups, half, rows, _ = slots.shape
+    count = groups * rows
+    total = probe.shape[1]
+    several = offsets.shape[0]
+    many = several * SPLIT
     steps = peers.bit_length() - 1
+    moments = (many, peers, RANK // SPLIT, total // peers)
+    packed = (steps, several * RANK // 2, 2 * RANK)
     vmem = pl.BlockSpec(memory_space=pltpu.VMEM)
     dma = pltpu.SemaphoreType.DMA
     return pl.pallas_call(
         functools.partial(reduce_kernel, peers),
         name="reduced",
         out_shape=(
-            jax.ShapeDtypeStruct(moments.shape, BF16),
-            jax.ShapeDtypeStruct(grams.shape, F32),
+            jax.ShapeDtypeStruct((several, count, total), BF16),
+            jax.ShapeDtypeStruct((several, count, RANK), BF16),
+            jax.ShapeDtypeStruct(moments, BF16),
+            jax.ShapeDtypeStruct((several, RANK, RANK), F32),
         ),
-        in_specs=[vmem] * 2,
-        out_specs=(vmem, vmem),
+        in_specs=[pl.BlockSpec(memory_space=pltpu.SMEM)] + [vmem] * 4,
+        out_specs=(vmem,) * 4,
         scratch_shapes=[
-            pltpu.VMEM(moments.shape, BF16),
-            pltpu.VMEM(moments.shape, BF16),
-            pltpu.VMEM((steps, grams.shape[0] * RANK // 2, 2 * RANK), F32),
-            pltpu.VMEM((steps, grams.shape[0] * RANK // 2, 2 * RANK), F32),
+            pltpu.VMEM((half, count, 2 * LANES), BF16),
+            pltpu.VMEM((half * count, 2 * LANES), F32),
+            pltpu.VMEM((half, count, 2 * LANES), F32),
+            pltpu.VMEM(moments, BF16),
+            pltpu.VMEM(moments, BF16),
+            pltpu.VMEM(moments, BF16),
+            pltpu.VMEM(packed, F32),
+            pltpu.VMEM(packed, F32),
         ]
         + [dma((many, steps))] * 4
         + [dma((steps,))] * 2,
         compiler_params=pltpu.CompilerParams(collective_id=1, has_side_effects=True),
-    )(moments, grams)
+    )(offsets, slots, backward, twists, probe)
 
 
 def project_kernel(sketch_ref, inverse_ref, moment_ref, out_ref):
@@ -515,10 +518,9 @@
     assert WINDOW == 4 * count and peers % 4 == 0
     forward, backward, twists = tables(total)
     slots = spectra(traces, alive, forward, twists, peers)
-    correlations, sketches, grams, moments = panels(
+    correlations, sketches, moments, inverses = reduced(
         offsets, slots, backward, twists, probe.T, peers
     )
-    moments, inverses = reduced(moments, grams, peers)
     return (correlations, projected(sketches, inverses, moments))
 
 

time: 75.9 us -> 73.2 us (0.964)
  Pallas kernels: 75 us -> 71.2 us
  local copies, waits for them, and re-layouts: 0 us -> 1.15 us
    pallas_call x1 -> x0, Pallas kernels: 8.71 us -> none  [panels(): pl.pallas_call(panel_kernel, name='panels', grid=(many,), out_shape=(jax....]
    pallas_call x1, Pallas kernels: 38.4 us -> 43.2 us  [reduced(): pl.pallas_call(functools.partial(reduce_kernel, peers), name='reduced', o...]
    unnamed x0 -> x3, local copies, waits for them, and re-layouts: none -> 1.15 us
where the time goes in v3:
time: 73.2 us; the launch traced here: 73 us
  Pallas kernels  71.2 us (97%)
  local copies, waits for them, and re-layouts  1.15 us (2%)
    pallas_call x1, Pallas kernels, reduced(): pl.pallas_call(functools.partial(reduce_kernel, peers), name='reduced', o...  43.2 us
    pallas_call x1, Pallas kernels, spectra(): pl.pallas_call(functools.partial(spectra_kernel, peers), name='spectra',...  23.8 us
    pallas_call x1, Pallas kernels, projected(): pl.pallas_call(project_kernel, name='projected', grid=(many,), out_shape=...  4.21 us

profile of v3, /device:TPU:0, one launch (start us, length us, event | category | flops | bytes accessed | tf_op | source)
XLA Modules:
  0.0 73.0 jit_solution(15476825007395619010)
XLA Ops:
  0.6 23.8 %spectra.1.slots = bf16[6,4,17,16,256]{4,3,2,1,0:T(8,128)(2,1)} custom-call(bf16[64,4096]{1,0:T(8,128)(2,1)} %x_ref.1, s32[1,64]{1,0:T(1,128)} %bitcast.3, bf16[256,256]{1,0:T(8,128)(2,1)} %constant.6.clone.forward_ref, f32[2,17,1,128]{3,2,1,0:T(1,128)} %constant.8.clone.twist_ref), custom_call_target="tpu_custom_call" | custom-call | tf_op jit(solution)/shard_map/spectra/pallas_call | solution.py:225
  24.5 43.2 %reduced.1 = (bf16[3,64,4096]{2,1,0:T(8,128)(2,1)}, bf16[3,64,64]{2,1,0:T(8,128)(2,1)}, bf16[6,16,32,256]{3,2,1,0:T(8,128)(2,1)}, f32[3,64,64]{2,1,0:T(8,128)}) custom-call(s32[3]{0:T(128)} %offsets_ref.1, bf16[6,4,17,16,256]{4,3,2,1,0:T(8,128)(2,1)} %spectra.1.slots, bf16[256,256]{1,0:T(8,128)(2,1)} %constant.7.clone.backward_ref, ...), custom_call_target="tpu_custom_call" | custom-call | tf_op jit(solution)/shard_map/reduced/pallas_call | solution.py:456
  67.7 0.0 copy-start
  67.7 4.2 %projected.1 = bf16[3,64,4096]{2,1,0:T(8,128)(2,1)} custom-call(bf16[3,64,64]{2,1,0:T(8,128)(2,1)} %get-tuple-element.7.sketch_ref, f32[3,64,64]{2,1,0:T(8,128)} %get-tuple-element.8.inverse_ref, bf16[6,16,32,256]{3,2,1,0:T(8,128)(2,1)} %get-tuple-element.9.moment_ref), custom_call_target="tpu_custom_call" | custom-call | tf_op jit(solution)/shard_map/projected/pallas_call | solution.py:502
  71.9 0.0 copy-done
  71.9 1.1 %copy.10 = bf16[3,64,4096]{2,1,0:T(8,128)(2,1)} copy(bf16[3,64,4096]{2,1,0:T(8,128)(2,1)S(1)} %copy-done) | data formatting | bytes 3145728
Async XLA Ops:
  67.7 4.2 %copy-start = (bf16[3,64,4096]{2,1,0:T(8,128)(2,1)S(1)}, bf16[3,64,4096]{2,1,0:T(8,128)(2,1)}, u32[]{:S(2)}) copy-start(bf16[3,64,4096]{2,1,0:T(8,128)(2,1)} %get-tuple-element.12) | copy-start | bytes 4718596

commit v4 on v3

--- a/solution.py
+++ b/solution.py
@@ -14,6 +14,7 @@
 LANES = 128
 ROWS = 16
 SPLIT = 2
+PIECES = 2
 OTHERS = (0, 3)
 F32 = jnp.float32
 BF16 = jnp.bfloat16
@@ -141,8 +142,8 @@
 
     def move(source, target, send, recv, index, peer):
         return pltpu.make_async_remote_copy(
-            src_ref=slots.at[source, index],
-            dst_ref=slots.at[target, index],
+            src_ref=slots.at[source, index // PIECES, pl.ds(*spans[index % PIECES])],
+            dst_ref=slots.at[target, index // PIECES, pl.ds(*spans[index % PIECES])],
             send_sem=send.at[index],
             recv_sem=recv.at[index],
             device_id={"fibre": peer},
@@ -150,6 +151,8 @@
         )
 
     own, nearer, farther = core, 2 + core, 4 + core
+    cuts = [half * i // PIECES for i in range(PIECES + 1)]
+    spans = [(a, b - a) for a, b in zip(cuts[:-1], cuts[1:])]
     for index in range(groups):
         rows = slice(index * ROWS, (index + 1) * ROWS)
         x = [x_ref[rows, a * LANES : (a + 1) * LANES].astype(F32) for a in range(radix)]
@@ -178,15 +181,16 @@
             met = 2 + has_upper.astype(jnp.int32) + has_lower.astype(jnp.int32)
             pl.semaphore_wait(barrier, met)
 
-        @pl.when(has_lower)
-        def _():
-            move(own, farther, z_s, z_r, index, lower).start()
-
-        @pl.when(odd == 1)
-        def _():
-            move(own, nearer, y_s, y_r, index, across).start()
-
-        move(own, own, core_s, core_r, index, pair).start()
+        for piece in range(index * PIECES, (index + 1) * PIECES):
+            @pl.when(has_lower)
+            def _():
+                move(own, farther, z_s, z_r, piece, lower).start()
+
+            @pl.when(odd == 1)
+            def _():
+                move(own, nearer, y_s, y_r, piece, across).start()
+
+            move(own, own, core_s, core_r, piece, pair).start()
 
     @pl.when(jnp.logical_not(has_upper))
     def _():
@@ -194,7 +198,7 @@
             for k in range(half):
                 slots[farther, index, k] = jnp.zeros((ROWS, 2 * LANES), BF16)
 
-    for index in range(groups):
+    for index in range(groups * PIECES):
         @pl.when(has_upper)
         def _():
             move(own, farther, z_s, z_r, index, lower).wait_recv()
@@ -206,7 +210,7 @@
         move(farther, farther, done_s, done_r, index, pair).start()
         move(own, nearer, y_s, y_r, index, across).wait_recv()
         move(nearer, nearer, relay_s, relay_r, index, pair).start()
-    for index in range(groups):
+    for index in range(groups * PIECES):
         move(own, own, core_s, core_r, index, pair).wait()
         move(farther, farther, done_s, done_r, index, pair).wait()
         move(nearer, nearer, relay_s, relay_r, index, pair).wait()
@@ -232,7 +236,7 @@
             pltpu.VMEM((half, ROWS, 2 * LANES), BF16),
             pltpu.VMEM((half * ROWS, 2 * LANES), F32),
         ]
-        + [pltpu.SemaphoreType.DMA((groups,))] * 10,
+        + [pltpu.SemaphoreType.DMA((groups * PIECES,))] * 10,
         compiler_params=pltpu.CompilerParams(collective_id=0, has_side_effects=True),
     )(traces, alive.reshape(1, count), forward, twists)
 

time: 73.2 us -> 72 us (0.984)
  Pallas kernels: 71.2 us -> 70 us
    pallas_call x1, Pallas kernels: 23.8 us -> 22.8 us  [spectra(): pl.pallas_call(functools.partial(spectra_kernel, peers), name='spectra',...]
where the time goes in v4:
time: 72 us; the launch traced here: 71.8 us
  Pallas kernels  70 us (97%)
  local copies, waits for them, and re-layouts  1.15 us (2%)
    pallas_call x1, Pallas kernels, reduced(): pl.pallas_call(functools.partial(reduce_kernel, peers), name='reduced', o...  43 us
    pallas_call x1, Pallas kernels, spectra(): pl.pallas_call(functools.partial(spectra_kernel, peers), name='spectra',...  22.8 us
    pallas_call x1, Pallas kernels, projected(): pl.pallas_call(project_kernel, name='projected', grid=(many,), out_shape=...  4.22 us

profile of v4, /device:TPU:0, one launch (start us, length us, event | category | flops | bytes accessed | tf_op | source)
XLA Modules:
  0.0 71.8 jit_solution(3898318825441019290)
XLA Ops:
  0.6 22.8 %spectra.1.slots = bf16[6,4,17,16,256]{4,3,2,1,0:T(8,128)(2,1)} custom-call(bf16[64,4096]{1,0:T(8,128)(2,1)} %x_ref.1, s32[1,64]{1,0:T(1,128)} %bitcast.3, bf16[256,256]{1,0:T(8,128)(2,1)} %constant.6.clone.forward_ref, f32[2,17,1,128]{3,2,1,0:T(1,128)} %constant.8.clone.twist_ref), custom_call_target="tpu_custom_call" | custom-call | tf_op jit(solution)/shard_map/spectra/pallas_call | solution.py:229
  23.4 43.0 %reduced.1 = (bf16[3,64,4096]{2,1,0:T(8,128)(2,1)}, bf16[3,64,64]{2,1,0:T(8,128)(2,1)}, bf16[6,16,32,256]{3,2,1,0:T(8,128)(2,1)}, f32[3,64,64]{2,1,0:T(8,128)}) custom-call(s32[3]{0:T(128)} %offsets_ref.1, bf16[6,4,17,16,256]{4,3,2,1,0:T(8,128)(2,1)} %spectra.1.slots, bf16[256,256]{1,0:T(8,128)(2,1)} %constant.7.clone.backward_ref, ...), custom_call_target="tpu_custom_call" | custom-call | tf_op jit(solution)/shard_map/reduced/pallas_call | solution.py:460
  66.5 0.0 copy-start
  66.5 4.2 %projected.1 = bf16[3,64,4096]{2,1,0:T(8,128)(2,1)} custom-call(bf16[3,64,64]{2,1,0:T(8,128)(2,1)} %get-tuple-element.7.sketch_ref, f32[3,64,64]{2,1,0:T(8,128)} %get-tuple-element.8.inverse_ref, bf16[6,16,32,256]{3,2,1,0:T(8,128)(2,1)} %get-tuple-element.9.moment_ref), custom_call_target="tpu_custom_call" | custom-call | tf_op jit(solution)/shard_map/projected/pallas_call | solution.py:506
  70.7 0.0 copy-done
  70.7 1.1 %copy.10 = bf16[3,64,4096]{2,1,0:T(8,128)(2,1)} copy(bf16[3,64,4096]{2,1,0:T(8,128)(2,1)S(1)} %copy-done) | data formatting | bytes 3145728
Async XLA Ops:
  66.5 4.2 %copy-start = (bf16[3,64,4096]{2,1,0:T(8,128)(2,1)S(1)}, bf16[3,64,4096]{2,1,0:T(8,128)(2,1)}, u32[]{:S(2)}) copy-start(bf16[3,64,4096]{2,1,0:T(8,128)(2,1)} %get-tuple-element.12) | copy-start | bytes 4718596
